TPU v7x, 32 devices: a whole 2x2x4 slice. The times are simulated.
32 devices in a mesh: patch: 2 (over x), epoch: 16 (over z, y, core).
Axes of the slice: x: 2, y: 2, z: 4, core: 2. Of those that a mesh axis runs over, the one named last changes fastest.
Arguments:
- images: float32 [32, 128, 1024], P(('patch', 'epoch')), parts along dimension 0, may hold values from -20 to 20, as said below
- variance: float32 [32], P(('patch', 'epoch')), parts along dimension 0, may hold values from 0.25 to 4
- zero_point: float32 [32], P(('patch', 'epoch')), parts along dimension 0, may hold values from 0.5 to 2
- block_mask: int32 [32, 1], P(('patch', 'epoch')), parts along dimension 0, may hold values 0 or 1
- stamps: int32 [32, 512], P(('patch', 'epoch')), parts along dimension 0, may hold values from 0 to 131071
- owners: int32 [8], P('patch'), parts along dimension 0, may hold values from 0 to 15
Outputs:
- significance: float32 [32, 128, 1024], P(('patch', 'epoch')), parts along dimension 0
- coefficients: float32 [32, 15], P(('patch', 'epoch')), parts along dimension 0
There are 2 independent parts, one for each index of `patch`. A program takes and returns all parts, laid end to end along the dimension named above; each array names one. Nothing has to cross between parts.
Inputs may be any that keep to these rules, and one draw needn't show every extreme that they name: `images`: each epoch is a common sky times an epoch scale plus noise.
All inputs are finite; a program needn't handle non-finite values. No bound on the sum of `block_mask` on one device may be relied on, other than what follows from the above.
Results may differ from a plain program's by a relative error of at most 0.00075.
The roundings to bfloat16 on the way count: a program that leaves them out, or rounds other values in their place, can miss the bound.
Values sent between devices are 32-bit elements; how exact they have to be, the bound alone decides.
A program may use at most 64 MiB of HBM per device.

v0:
```python
import math
import jax
import jax.numpy as jnp
from jax import lax
from jax.sharding import PartitionSpec as P

TILES = 4
KHALF = 7
NBASIS = 12
sigma_list = (0.75, 1.5, 3.0)
basis_pairs = ((0, 0), (2, 0), (0, 2), (1, 1))


def raise_power(scaled, degree):
    result = jnp.ones_like(scaled)
    for step in range(degree):
        result = result * scaled
    return result


def tap_values(offset, sigma, degree):
    scaled = offset / sigma
    value = (
        jnp.exp(-0.5 * scaled * scaled)
        * raise_power(scaled, degree)
        / (math.sqrt(2.0 * math.pi) * sigma)
    )
    value = jnp.where(jnp.abs(offset) <= KHALF, value, 0.0)
    return value.astype(jnp.bfloat16)


def band_matrix(count, sigma, degree, along_cols):
    index = jnp.arange(count, dtype=jnp.int32)
    if along_cols:
        offset = index[:, None] - index[None, :]
    else:
        offset = index[None, :] - index[:, None]
    return tap_values(offset.astype(jnp.float32), sigma, degree)


def shards(images, variance, zero_point, block_mask, stamps, owners):
    image = images[0]
    rows_all, cols_all = image.shape
    count = lax.axis_size("epoch")
    weight = 1.0 / variance[0]
    mask_f = block_mask[0].astype(jnp.float32)
    block_term = weight * mask_f
    numer = jnp.repeat(block_term, 128)[:, None] * image
    scales_all = lax.all_gather(zero_point, "epoch", axis=0, tiled=True)
    owner_scale = jnp.sum(
        (owners[:, None] == jnp.arange(count)[None, :]).astype(jnp.float32) * scales_all[None, :],
        axis=1,
    )
    col_scale = jnp.repeat(owner_scale, cols_all // TILES)
    stamp_row = stamps[0]
    numer_sum, block_sum = lax.psum((numer, block_term), "epoch")
    den_rows = jnp.repeat(1.0 + block_sum, 128)
    reference_img = numer_sum / den_rows[:, None] * col_scale[None, :]
    stamp_ref = jnp.take(reference_img.reshape(-1), stamp_row)
    sharp = image.astype(jnp.bfloat16)
    bases = []
    for sigma in sigma_list:
        across = {}
        for degree in (0, 1, 2):
            across[degree] = jnp.dot(
                sharp,
                band_matrix(cols_all, sigma, degree, True),
                preferred_element_type=jnp.float32,
            ).astype(jnp.bfloat16)
        for pair in basis_pairs:
            vertical = band_matrix(rows_all, sigma, pair[1], False)
            bases.append(
                jnp.dot(vertical, across[pair[0]], preferred_element_type=jnp.float32).astype(
                    jnp.bfloat16
                )
            )
    xn = 2.0 * (jnp.arange(cols_all).astype(jnp.float32) + 0.5) / cols_all - 1.0
    yn = 2.0 * (jnp.arange(rows_all).astype(jnp.float32) + 0.5) / rows_all - 1.0
    picks = [jnp.take(b.reshape(-1), stamp_row).astype(jnp.float32) for b in bases]
    picks = picks + [
        jnp.ones(stamp_row.shape, jnp.float32),
        xn[stamp_row % cols_all],
        yn[stamp_row // cols_all],
    ]
    design = jnp.stack(picks, axis=0)
    normal = jnp.dot(design, design.T, precision=lax.Precision.HIGHEST)
    normal = normal + 0.05 * jnp.diag(jnp.diag(normal))
    rhs = jnp.dot(design, stamp_ref, precision=lax.Precision.HIGHEST)
    factor = jnp.linalg.cholesky(normal)
    coef = jax.scipy.linalg.cho_solve((factor, True), rhs)
    model = jnp.zeros((rows_all, cols_all), jnp.float32)
    for index in range(NBASIS):
        model = model + coef[index] * bases[index].astype(jnp.float32)
    model = model + coef[NBASIS] + coef[NBASIS + 1] * xn[None, :] + coef[NBASIS + 2] * yn[:, None]
    diff = jnp.repeat(mask_f, 128)[:, None] * (model - reference_img)
    pooled = lax.psum(diff * diff, "epoch")
    scatter = jnp.sqrt(0.05 + pooled / count)
    result = diff / scatter
    return (result[None], coef[None])


def solution(mesh):
    in_specs = (
        P(("patch", "epoch"), None, None),
        P(("patch", "epoch")),
        P(("patch", "epoch")),
        P(("patch", "epoch"), None),
        P(("patch", "epoch"), None),
        P("patch"),
    )
    out_specs = (P(("patch", "epoch"), None, None), P(("patch", "epoch"), None))
    return jax.shard_map(shards, mesh=mesh, in_specs=in_specs, out_specs=out_specs, check_vma=False)
```

profile of v0, /device:TPU:0, one launch (start us, length us, event | category | flops | bytes accessed | tf_op | source)
XLA Modules:
  0.0 242.0 jit_solution(10815017619409974044)
XLA Ops:
  7.2 0.0 all-reduce.5.cloned.1.call-start
  8.5 2.2 fusion.182
  10.7 0.0 all-reduce.5.cloned.1.call-update
  10.8 0.0 all-reduce.7.cloned.1.call-start
  10.8 2.3 fusion.11
  13.1 2.2 fusion.15
  15.3 2.4 fusion.14
  17.7 0.2 convolution_convert_fusion
  17.9 0.2 convolution_convert_fusion.1
  18.2 2.3 fusion.18
  20.5 2.2 fusion.22
  22.6 2.6 %fusion.21 = bf16[128,1024]{1,0:T(8,128)(2,1)S(1)} fusion(bf16[1,128,1024]{2,1,0:T(8,128)(2,1)S(1)} %get-tuple-element.11), kind=kOutput, calls=%fused_computation.54 | convolution fusion | flops 314998784 | bytes 524288 | tf_op jit(solution)/shard_map/dot_general | solution.py:73
  25.2 0.0 copy-start.1
  25.2 0.2 convolution_convert_fusion.2
  25.5 0.2 convolution_convert_fusion.3
  25.7 3.0 %fusion.25 = bf16[128,1024]{1,0:T(8,128)(2,1)} fusion(bf16[1,128,1024]{2,1,0:T(8,128)(2,1)S(1)} %get-tuple-element.11), kind=kOutput, calls=%fused_computation.58 | convolution fusion | flops 313966592 | bytes 524288 | tf_op jit(solution)/shard_map/dot_general | solution.py:73
  28.7 2.2 fusion.29
  30.9 3.1 %fusion.28 = bf16[128,1024]{1,0:T(8,128)(2,1)} fusion(bf16[1,128,1024]{2,1,0:T(8,128)(2,1)S(1)} %get-tuple-element.11), kind=kOutput, calls=%fused_computation.61 | convolution fusion | flops 314998784 | bytes 524288 | tf_op jit(solution)/shard_map/dot_general | solution.py:73
  34.0 0.2 convolution_convert_fusion.4
  34.2 0.2 convolution_convert_fusion.5
  35.1 0.6 dynamic-slice
  35.7 0.8 dynamic-update-slice.3
  36.5 36.3 %all-reduce.1 = (f32[16]{0:T(128)S(1)}, f32[1]{0:T(128)}) all-reduce(f32[16]{0:T(128)S(1)} %dynamic-update-slice.3, f32[1]{0:T(128)} %mul.385), channel_id=1, replica_groups=mesh['patch'=2,'epoch'=16] {'epoch'}, use_global_device_ids=true, to_apply=%add | all-reduce | flops 17 | bytes 136
  72.8 0.2 select_reduce_fusion.1
  72.9 0.1 broadcast_bitcast_fusion
  73.9 3.5 %gather_fusion.15 = bf16[512]{0:T(512)(128)(2,1)S(1)} fusion(bf16[131072]{0:T(1024)(128)(2,1)S(1)} %bitcast.149, s32[1024]{0:T(1024)S(1)} %pad_clamp_fusion.3), kind=kCustom, calls=%fused_computation.11.clone | custom fusion | bytes 4096 | tf_op jit(solution)/shard_map/jit(_take)/gather | solution.py:79
  77.4 3.5 %gather_fusion.14 = bf16[512]{0:T(512)(128)(2,1)S(1)} fusion(bf16[131072]{0:T(1024)(128)(2,1)S(1)} %bitcast.148, s32[1024]{0:T(1024)S(1)} %pad_clamp_fusion.3), kind=kCustom, calls=%fused_computation.10.clone | custom fusion | bytes 4096 | tf_op jit(solution)/shard_map/jit(_take)/gather | solution.py:79
  81.0 3.5 %gather_fusion.13 = bf16[512]{0:T(512)(128)(2,1)S(1)} fusion(bf16[131072]{0:T(1024)(128)(2,1)S(1)} %bitcast.151, s32[1024]{0:T(1024)S(1)} %pad_clamp_fusion.3), kind=kCustom, calls=%fused_computation.9.clone | custom fusion | bytes 4096 | tf_op jit(solution)/shard_map/jit(_take)/gather | solution.py:79
  84.6 3.5 %gather_fusion.12 = bf16[512]{0:T(512)(128)(2,1)S(1)} fusion(bf16[131072]{0:T(1024)(128)(2,1)S(1)} %bitcast.152, s32[1024]{0:T(1024)S(1)} %pad_clamp_fusion.3), kind=kCustom, calls=%fused_computation.8.clone | custom fusion | bytes 4096 | tf_op jit(solution)/shard_map/jit(_take)/gather | solution.py:79
  88.1 3.5 %gather_fusion.11 = bf16[512]{0:T(512)(128)(2,1)S(1)} fusion(bf16[131072]{0:T(1024)(128)(2,1)S(1)} %bitcast.153, s32[1024]{0:T(1024)S(1)} %pad_clamp_fusion.3), kind=kCustom, calls=%fused_computation.7.clone | custom fusion | bytes 4096 | tf_op jit(solution)/shard_map/jit(_take)/gather | solution.py:79
  91.7 3.5 %gather_fusion.10 = bf16[512]{0:T(512)(128)(2,1)S(1)} fusion(bf16[131072]{0:T(1024)(128)(2,1)S(1)} %bitcast.154, s32[1024]{0:T(1024)S(1)} %pad_clamp_fusion.3), kind=kCustom, calls=%fused_computation.6.clone | custom fusion | bytes 4096 | tf_op jit(solution)/shard_map/jit(_take)/gather | solution.py:79
  95.3 3.5 %gather_fusion.9 = bf16[512]{0:T(512)(128)(2,1)S(1)} fusion(bf16[131072]{0:T(1024)(128)(2,1)S(1)} %bitcast.155, s32[1024]{0:T(1024)S(1)} %pad_clamp_fusion.3), kind=kCustom, calls=%fused_computation.5.clone | custom fusion | bytes 4096 | tf_op jit(solution)/shard_map/jit(_take)/gather | solution.py:79
  98.9 0.0 copy-start.2
  98.9 3.5 %gather_fusion.8 = bf16[512]{0:T(512)(128)(2,1)S(1)} fusion(bf16[131072]{0:T(1024)(128)(2,1)S(1)} %bitcast.156, s32[1024]{0:T(1024)S(1)} %pad_clamp_fusion.3), kind=kCustom, calls=%fused_computation.4.clone | custom fusion | bytes 4096 | tf_op jit(solution)/shard_map/jit(_take)/gather | solution.py:79
  102.5 3.5 %gather_fusion.7 = bf16[512]{0:T(512)(128)(2,1)S(1)} fusion(bf16[131072]{0:T(1024)(128)(2,1)S(1)} %bitcast.157, s32[1024]{0:T(1024)S(1)} %pad_clamp_fusion.3), kind=kCustom, calls=%fused_computation.3.clone | custom fusion | bytes 4096 | tf_op jit(solution)/shard_map/jit(_take)/gather | solution.py:79
  106.0 3.5 %gather_fusion.6 = bf16[512]{0:T(512)(128)(2,1)S(1)} fusion(bf16[131072]{0:T(1024)(128)(2,1)S(1)} %bitcast.158, s32[1024]{0:T(1024)S(1)} %pad_clamp_fusion.3), kind=kCustom, calls=%fused_computation.2.clone | custom fusion | bytes 4096 | tf_op jit(solution)/shard_map/jit(_take)/gather | solution.py:79
  109.6 3.5 %gather_fusion.5 = bf16[512]{0:T(512)(128)(2,1)S(1)} fusion(bf16[131072]{0:T(1024)(128)(2,1)S(1)} %bitcast.159, s32[1024]{0:T(1024)S(1)} %pad_clamp_fusion.3), kind=kCustom, calls=%fused_computation.1.clone | custom fusion | bytes 4096 | tf_op jit(solution)/shard_map/jit(_take)/gather | solution.py:79
  113.2 3.5 %gather_fusion.4 = bf16[512]{0:T(512)(128)(2,1)S(1)} fusion(bf16[131072]{0:T(1024)(128)(2,1)S(1)} %bitcast.150, s32[1024]{0:T(1024)S(1)} %pad_clamp_fusion.3), kind=kCustom, calls=%fused_computation.clone | custom fusion | bytes 4096 | tf_op jit(solution)/shard_map/jit(_take)/gather | solution.py:79
  116.7 2.3 gather_fusion
  119.0 3.3 %gather_fusion.1 = f32[512]{0:T(512)S(1)} fusion(f32[128]{0:T(128)S(1)} %multiply_add_fusion.1, s32[1024]{0:T(1024)S(1)} %pad_clamp_fusion.1), kind=kCustom, calls=%fused_computation.13 | custom fusion | bytes 6144 | tf_op jit(solution)/shard_map/gather | solution.py:83
  122.4 0.0 all-reduce.5.cloned.1.call-done
  122.4 1.1 fusion.45
  123.5 0.1 copy.24
  123.6 3.1 %gather_fusion.3 = f32[512]{0:T(512)S(1)} fusion(f32[131072]{0:T(1024)S(1)} %bitcast.147, s32[1024]{0:T(1024)S(1)} %pad_clamp_fusion), kind=kCustom, calls=%fused_computation.15 | custom fusion | bytes 6144 | tf_op jit(solution)/shard_map/jit(_take)/gather | solution.py:59
  126.8 0.0 copy-start
  126.8 0.1 stack.107
  126.9 0.1 fusion.184
  127.1 0.2 convolution_bitcast_fusion
  127.2 0.1 copy.10
  127.3 0.7 gather_fusion.2
  128.0 0.1 fusion.75
  128.1 1.4 cholesky.16
  129.5 0.6 compare_reduce_fusion
  130.2 0.6 fusion.70
  130.8 1.2 custom-call.10
  132.0 0.1 convolution_bitcast_fusion.1
  132.1 0.1 fusion.71
  132.3 0.7 fusion.183
  133.0 0.7 broadcast_multiply_fusion.1
  133.6 0.6 broadcast_multiply_fusion
  134.3 10.7 %fusion.181 = (f32[128,1024]{1,0:T(8,128)}, f32[128,1024]{1,0:T(8,128)S(1)}) fusion(f32[1024]{0:T(1024)S(1)} %bitcast.174, f32[128,1024]{1,0:T(8,128)S(1)} %copy-done, f32[]{:T(128)} %bitcast.27, f32[128]{0:T(128)S(1)} %broadcast_multiply_fusion.1, f32[1024]{0:T(1024)S(1)} %broadcast_multiply_fusion, f32[]{:T(128)} %bitcast.48, ...), kind=kLoop, calls=%fused_computation.250 | loop fusion | flops 5636096 | bytes 4727356 | tf_op jit(solution)/shard_map/mul | solution.py:96
  145.0 0.0 all-reduce.7.cloned.1.call-update
  145.0 88.2 %all-reduce.7.cloned.1.call-done = f32[128,1024]{1,0:T(8,128)} async-done(((f32[128,1024]{1,0:T(8,128)}), f32[128,1024]{1,0:T(8,128)}) %all-reduce.7.cloned.1.call-update) | async-done | bytes 524304 | tf_op jit(solution)/shard_map/psum | solution.py:96
  233.2 1.9 multiply_bitcast_fusion
  (41 shorter events, 0.7 us)
Async XLA Ops:
  7.2 115.3 %all-reduce.5.cloned.1.call-start = ((), (), s32[]{:S(2)}) async-start(), calls=%async_computation | async-start | bytes 1048576 | tf_op jit(solution)/shard_map/psum | solution.py:56
  10.8 222.4 %all-reduce.7.cloned.1.call-start = ((), (), s32[]{:S(2)}) async-start(), calls=%async_computation.1 | async-start | bytes 1048576 | tf_op jit(solution)/shard_map/psum | solution.py:96
  25.2 70.0 %copy-start.1 = (bf16[128,1024]{1,0:T(8,128)(2,1)}, bf16[128,1024]{1,0:T(8,128)(2,1)S(1)}, u32[]{:S(2)}) copy-start(bf16[128,1024]{1,0:T(8,128)(2,1)S(1)} %fusion.21) | copy-start | bytes 786436
  34.0 1.1 copy-start.7
  34.0 38.8 %copy-start.6 = (s32[4]{0:T(128)S(1)}, s32[4]{0:T(128)}, u32[]{:S(2)}) copy-start(s32[4]{0:T(128)} %param.13) | copy-start | bytes 52
  34.0 39.0 %copy-start.5 = (s32[1,512]{1,0:T(1,128)S(1)}, s32[1,512]{1,0:T(1,128)}, u32[]{:S(2)}) copy-start(s32[1,512]{1,0:T(1,128)} %param.12) | copy-start | bytes 6148
  98.9 3.5 %copy-start.2 = (bf16[128,1024]{1,0:T(8,128)(2,1)S(1)}, bf16[128,1024]{1,0:T(8,128)(2,1)}, u32[]{:S(2)}) copy-start(bf16[128,1024]{1,0:T(8,128)(2,1)} %fusion.25) | copy-start | bytes 786436
  106.0 3.5 %copy-start.3 = (bf16[128,1024]{1,0:T(8,128)(2,1)S(1)}, bf16[128,1024]{1,0:T(8,128)(2,1)}, u32[]{:S(2)}) copy-start(bf16[128,1024]{1,0:T(8,128)(2,1)} %fusion.28) | copy-start | bytes 786436
  126.8 7.5 %copy-start = (f32[128,1024]{1,0:T(8,128)S(1)}, f32[128,1024]{1,0:T(8,128)}, u32[]{:S(2)}) copy-start(f32[128,1024]{1,0:T(8,128)} %all-reduce.5.cloned.1.call-done) | copy-start | bytes 1572868
  132.3 12.7 %copy-start.4 = (f32[1,15]{1,0:T(1,128)}, f32[1,15]{1,0:T(1,128)S(1)}, u32[]{:S(2)}) copy-start(f32[1,15]{1,0:T(1,128)S(1)} %fusion.71) | copy-start | bytes 184
Sparse Core Ops, SparseCore 0:
  11.9 93.5 all-reduce.4
  145.1 88.0 all-reduce.6
where the time goes:
time: 242 us
  waiting for transfers between devices  88.2 us (36%)
  local copies, waits for them, and re-layouts  54.6 us (23%)
  blocking collectives  36.3 us (15%)
  matrix products  24.1 us (10%)
  other arithmetic  21.4 us (9%)
  between operations  17.2 us (7%)
    psum x1, waiting for transfers between devices, shards(): pooled = lax.psum(diff * diff, 'epoch')  88.2 us
    gather x12, local copies, waits for them, and re-layouts, shards(): jnp.take(b.reshape(-1), stamp_row).astype(jnp.float32)  42.2 us
    unnamed x1, blocking collectives  36.3 us
    dot_general x12, matrix products, shards(): jnp.dot(vertical, across[pair[0]], preferred_element_type=jnp.float32)  17 us
    mul x1, other arithmetic, shards(): pooled = lax.psum(diff * diff, 'epoch')  10.7 us
    dot_general x3, matrix products, shards(): jnp.dot(sharp, band_matrix(cols_all, sigma, degree, True), preferred_elem...  6.5 us
  transfers between devices with their start and end apart: 2, of which 1 were waited for; matrix products, arithmetic and copies ran while one was open for 30% of the time, Pallas kernels for 0%

commit v1 on v0

--- a/solution.py
+++ b/solution.py
@@ -3,6 +3,7 @@
 import jax.numpy as jnp
 from jax import lax
 from jax.sharding import PartitionSpec as P
+from jax.lax import all_gather
 
 TILES = 4
 KHALF = 7
@@ -93,7 +94,13 @@
         model = model + coef[index] * bases[index].astype(jnp.float32)
     model = model + coef[NBASIS] + coef[NBASIS + 1] * xn[None, :] + coef[NBASIS + 2] * yn[:, None]
     diff = jnp.repeat(mask_f, 128)[:, None] * (model - reference_img)
-    pooled = lax.psum(diff * diff, "epoch")
+
+    def wrap_the_cards(own_rows):
+        latest = all_gather(own_rows, "epoch")
+        fresh = jnp.sum(latest, axis=0)
+        return fresh
+
+    pooled = wrap_the_cards(diff * diff)
     scatter = jnp.sqrt(0.05 + pooled / count)
     result = diff / scatter
     return (result[None], coef[None])

time: 242 us -> 229 us (0.946)
  waiting for transfers between devices: 88.2 us -> 71.8 us
  other arithmetic: 21.4 us -> 24.6 us
    psum x1 -> x0, waiting for transfers between devices: 88.2 us -> none  [shards(): pooled = lax.psum(diff * diff, 'epoch')]
    all_gather x0 -> x1, waiting for transfers between devices: none -> 71.7 us  [wrap_the_cards(): latest = all_gather(own_rows, 'epoch')]
    reduce_sum x0 -> x1, other arithmetic: none -> 4.24 us  [wrap_the_cards(): fresh = jnp.sum(latest, axis=0)]
  transfers between devices with their start and end apart: 2 -> 2, of which waited for: 1 -> 1; matrix products, arithmetic and copies ran while one was open for 30% -> 32% of each run, Pallas kernels for 0% -> 0%
where the time goes in v1:
time: 229 us
  waiting for transfers between devices  71.8 us (31%)
  local copies, waits for them, and re-layouts  55.6 us (24%)
  blocking collectives  36.3 us (16%)
  other arithmetic  24.6 us (11%)
  matrix products  23.4 us (10%)
  between operations  17.2 us (8%)
    all_gather x1, waiting for transfers between devices, wrap_the_cards(): latest = all_gather(own_rows, 'epoch')  71.7 us
    gather x12, local copies, waits for them, and re-layouts, shards(): jnp.take(b.reshape(-1), stamp_row).astype(jnp.float32)  42.2 us
    unnamed x1, blocking collectives  36.3 us
    dot_general x12, matrix products, shards(): jnp.dot(vertical, across[pair[0]], preferred_element_type=jnp.float32)  16.1 us
    mul x1, other arithmetic, shards(): pooled = wrap_the_cards(diff * diff)  10.7 us
    dot_general x3, matrix products, shards(): jnp.dot(sharp, band_matrix(cols_all, sigma, degree, True), preferred_elem...  6.67 us
  transfers between devices with their start and end apart: 2, of which 1 were waited for; matrix products, arithmetic and copies ran while one was open for 32% of the time, Pallas kernels for 0%

profile of v1, /device:TPU:0, one launch (start us, length us, event | category | flops | bytes accessed | tf_op | source)
XLA Modules:
  0.0 228.9 jit_solution(13769973543355352366)
XLA Ops:
  7.2 0.0 all-reduce.4.cloned.1.call-start
  8.5 2.1 fusion.182
  10.6 0.0 all-reduce.4.cloned.1.call-update
  10.7 0.0 all-gather.3.cloned.1.call-start
  10.7 2.4 %fusion.28 = bf16[128,1024]{1,0:T(8,128)(2,1)S(1)} fusion(bf16[1,128,1024]{2,1,0:T(8,128)(2,1)S(1)} %get-tuple-element.11), kind=kOutput, calls=%fused_computation.61 | convolution fusion | flops 314998784 | bytes 524288 | tf_op jit(solution)/shard_map/dot_general | solution.py:74
  13.1 2.3 fusion.25
  15.4 2.2 fusion.22
  17.6 0.2 convolution_convert_fusion.2
  17.8 0.2 convolution_convert_fusion.3
  18.1 2.4 %fusion.21 = bf16[128,1024]{1,0:T(8,128)(2,1)S(1)} fusion(bf16[1,128,1024]{2,1,0:T(8,128)(2,1)S(1)} %get-tuple-element.11), kind=kOutput, calls=%fused_computation.54 | convolution fusion | flops 314998784 | bytes 524288 | tf_op jit(solution)/shard_map/dot_general | solution.py:74
  20.5 2.3 fusion.18
  22.8 2.3 %fusion.15 = bf16[1024,128]{1,0:T(8,128)(2,1)S(1)} fusion(bf16[1,128,1024]{2,1,0:T(8,128)(2,1)S(1)} %get-tuple-element.11), kind=kOutput, calls=%fused_computation.48 | convolution fusion | flops 279052288 | bytes 524288 | tf_op jit(solution)/shard_map/dot_general | solution.py:66
  25.1 0.2 convolution_convert_fusion
  25.4 0.2 convolution_convert_fusion.1
  25.6 2.4 %fusion.14 = bf16[128,1024]{1,0:T(8,128)(2,1)S(1)} fusion(bf16[1,128,1024]{2,1,0:T(8,128)(2,1)S(1)} %get-tuple-element.11), kind=kOutput, calls=%fused_computation.47 | convolution fusion | flops 314998784 | bytes 524288 | tf_op jit(solution)/shard_map/dot_general | solution.py:74
  28.0 3.0 %fusion.11 = bf16[128,1024]{1,0:T(8,128)(2,1)} fusion(bf16[1,128,1024]{2,1,0:T(8,128)(2,1)S(1)} %get-tuple-element.11), kind=kOutput, calls=%fused_computation.44 | convolution fusion | flops 313966592 | bytes 524288 | tf_op jit(solution)/shard_map/dot_general | solution.py:74
  31.0 2.2 fusion.29
  33.2 0.2 convolution_convert_fusion.4
  33.4 0.2 convolution_convert_fusion.5
  34.3 0.6 dynamic-slice
  34.9 0.8 dynamic-update-slice.3
  35.7 36.3 %all-reduce.1 = (f32[16]{0:T(128)S(1)}, f32[1]{0:T(128)}) all-reduce(f32[16]{0:T(128)S(1)} %dynamic-update-slice.3, f32[1]{0:T(128)} %mul.385), channel_id=1, replica_groups=mesh['patch'=2,'epoch'=16] {'epoch'}, use_global_device_ids=true, to_apply=%add | all-reduce | flops 17 | bytes 136
  72.1 0.2 select_reduce_fusion.1
  72.3 0.1 broadcast_bitcast_fusion
  73.1 3.5 %gather_fusion.6 = bf16[512]{0:T(512)(128)(2,1)S(1)} fusion(bf16[131072]{0:T(1024)(128)(2,1)S(1)} %bitcast.151, s32[1024]{0:T(1024)S(1)} %pad_clamp_fusion.3), kind=kCustom, calls=%fused_computation.2.clone | custom fusion | bytes 4096 | tf_op jit(solution)/shard_map/jit(_take)/gather | solution.py:80
  76.7 3.5 %gather_fusion.4 = bf16[512]{0:T(512)(128)(2,1)S(1)} fusion(bf16[131072]{0:T(1024)(128)(2,1)S(1)} %bitcast.150, s32[1024]{0:T(1024)S(1)} %pad_clamp_fusion.3), kind=kCustom, calls=%fused_computation.clone | custom fusion | bytes 4096 | tf_op jit(solution)/shard_map/jit(_take)/gather | solution.py:80
  80.2 1.0 copy.22
  81.2 3.5 %gather_fusion.15 = bf16[512]{0:T(512)(128)(2,1)S(1)} fusion(bf16[131072]{0:T(1024)(128)(2,1)S(1)} %bitcast.153, s32[1024]{0:T(1024)S(1)} %pad_clamp_fusion.3), kind=kCustom, calls=%fused_computation.11.clone | custom fusion | bytes 4096 | tf_op jit(solution)/shard_map/jit(_take)/gather | solution.py:80
  84.7 0.0 copy-done.2
  84.8 3.5 %gather_fusion.13 = bf16[512]{0:T(512)(128)(2,1)S(1)} fusion(bf16[131072]{0:T(1024)(128)(2,1)S(1)} %bitcast.154, s32[1024]{0:T(1024)S(1)} %pad_clamp_fusion.3), kind=kCustom, calls=%fused_computation.9.clone | custom fusion | bytes 4096 | tf_op jit(solution)/shard_map/jit(_take)/gather | solution.py:80
  88.3 3.5 %gather_fusion.14 = bf16[512]{0:T(512)(128)(2,1)S(1)} fusion(bf16[131072]{0:T(1024)(128)(2,1)S(1)} %bitcast.155, s32[1024]{0:T(1024)S(1)} %pad_clamp_fusion.3), kind=kCustom, calls=%fused_computation.10.clone | custom fusion | bytes 4096 | tf_op jit(solution)/shard_map/jit(_take)/gather | solution.py:80
  91.9 3.5 %gather_fusion.12 = bf16[512]{0:T(512)(128)(2,1)S(1)} fusion(bf16[131072]{0:T(1024)(128)(2,1)S(1)} %bitcast.156, s32[1024]{0:T(1024)S(1)} %pad_clamp_fusion.3), kind=kCustom, calls=%fused_computation.8.clone | custom fusion | bytes 4096 | tf_op jit(solution)/shard_map/jit(_take)/gather | solution.py:80
  95.5 3.5 %gather_fusion.11 = bf16[512]{0:T(512)(128)(2,1)S(1)} fusion(bf16[131072]{0:T(1024)(128)(2,1)S(1)} %bitcast.157, s32[1024]{0:T(1024)S(1)} %pad_clamp_fusion.3), kind=kCustom, calls=%fused_computation.7.clone | custom fusion | bytes 4096 | tf_op jit(solution)/shard_map/jit(_take)/gather | solution.py:80
  99.1 3.5 %gather_fusion.9 = bf16[512]{0:T(512)(128)(2,1)S(1)} fusion(bf16[131072]{0:T(1024)(128)(2,1)S(1)} %bitcast.158, s32[1024]{0:T(1024)S(1)} %pad_clamp_fusion.3), kind=kCustom, calls=%fused_computation.5.clone | custom fusion | bytes 4096 | tf_op jit(solution)/shard_map/jit(_take)/gather | solution.py:80
  102.6 3.5 %gather_fusion.10 = bf16[512]{0:T(512)(128)(2,1)S(1)} fusion(bf16[131072]{0:T(1024)(128)(2,1)S(1)} %bitcast.159, s32[1024]{0:T(1024)S(1)} %pad_clamp_fusion.3), kind=kCustom, calls=%fused_computation.6.clone | custom fusion | bytes 4096 | tf_op jit(solution)/shard_map/jit(_take)/gather | solution.py:80
  106.2 3.5 %gather_fusion.8 = bf16[512]{0:T(512)(128)(2,1)S(1)} fusion(bf16[131072]{0:T(1024)(128)(2,1)S(1)} %bitcast.160, s32[1024]{0:T(1024)S(1)} %pad_clamp_fusion.3), kind=kCustom, calls=%fused_computation.4.clone | custom fusion | bytes 4096 | tf_op jit(solution)/shard_map/jit(_take)/gather | solution.py:80
  109.8 3.5 %gather_fusion.7 = bf16[512]{0:T(512)(128)(2,1)S(1)} fusion(bf16[131072]{0:T(1024)(128)(2,1)S(1)} %bitcast.161, s32[1024]{0:T(1024)S(1)} %pad_clamp_fusion.3), kind=kCustom, calls=%fused_computation.3.clone | custom fusion | bytes 4096 | tf_op jit(solution)/shard_map/jit(_take)/gather | solution.py:80
  113.4 3.5 %gather_fusion.5 = bf16[512]{0:T(512)(128)(2,1)S(1)} fusion(bf16[131072]{0:T(1024)(128)(2,1)S(1)} %bitcast.152, s32[1024]{0:T(1024)S(1)} %pad_clamp_fusion.3), kind=kCustom, calls=%fused_computation.1.clone | custom fusion | bytes 4096 | tf_op jit(solution)/shard_map/jit(_take)/gather | solution.py:80
  116.9 3.3 %gather_fusion.1 = f32[512]{0:T(512)S(1)} fusion(f32[128]{0:T(128)S(1)} %multiply_add_fusion.1, s32[1024]{0:T(1024)S(1)} %pad_clamp_fusion.1), kind=kCustom, calls=%fused_computation.13 | custom fusion | bytes 6144 | tf_op jit(solution)/shard_map/gather | solution.py:84
  120.2 2.3 gather_fusion
  122.6 0.0 all-reduce.4.cloned.1.call-done
  122.6 1.2 fusion.45
  123.8 0.1 copy.24
  123.9 3.1 %gather_fusion.3 = f32[512]{0:T(512)S(1)} fusion(f32[131072]{0:T(1024)S(1)} %bitcast.148, s32[1024]{0:T(1024)S(1)} %pad_clamp_fusion), kind=kCustom, calls=%fused_computation.15 | custom fusion | bytes 6144 | tf_op jit(solution)/shard_map/jit(_take)/gather | solution.py:60
  127.1 0.1 stack.107
  127.2 0.1 fusion.184
  127.3 0.2 convolution_bitcast_fusion
  127.5 0.1 copy.10
  127.5 0.7 gather_fusion.2
  128.3 0.1 fusion.75
  128.4 1.4 cholesky.16
  129.8 0.6 compare_reduce_fusion
  130.4 0.6 fusion.70
  131.1 1.2 custom-call.10
  132.2 0.1 convolution_bitcast_fusion.1
  132.3 0.1 fusion.71
  132.5 0.7 fusion.183
  133.2 0.7 broadcast_multiply_fusion.1
  133.9 0.6 broadcast_multiply_fusion
  134.5 10.7 %fusion.181 = (f32[128,1024]{1,0:T(8,128)}, f32[128,1024]{1,0:T(8,128)S(1)}) fusion(f32[1024]{0:T(1024)S(1)} %bitcast.176, f32[128,1024]{1,0:T(8,128)S(1)} %copy-done, f32[]{:T(128)} %bitcast.27, f32[128]{0:T(128)S(1)} %broadcast_multiply_fusion.1, f32[1024]{0:T(1024)S(1)} %broadcast_multiply_fusion, f32[]{:T(128)} %bitcast.48, ...), kind=kLoop, calls=%fused_computation.250 | loop fusion | flops 5636096 | bytes 4727356 | tf_op jit(solution)/shard_map/mul | solution.py:103
  145.2 0.0 all-gather.3.cloned.1.call-update
  145.3 71.7 %all-gather.3.cloned.1.call-done = f32[2048,1024]{1,0:T(8,128)} async-done(((f32[128,1024]{1,0:T(8,128)}), f32[2048,1024]{1,0:T(8,128)}) %all-gather.3.cloned.1.call-update) | async-done | bytes 8388624 | tf_op jit(solution)/shard_map/all_gather | solution.py:99
  217.0 4.2 %reduce_sum.19 = f32[128,1024]{1,0:T(8,128)S(1)} reduce(f32[16,128,1024]{2,1,0:T(8,128)} %bitcast.149, f32[]{:T(128)} %constant.175.clone.1), dimensions={0}, to_apply=%region_5.7 | reduce | flops 1966080 | bytes 8912900 | tf_op jit(solution)/shard_map/reduce_sum | solution.py:100
  221.2 0.9 multiply_bitcast_fusion
  (40 shorter events, 0.7 us)
Async XLA Ops:
  7.2 115.4 %all-reduce.4.cloned.1.call-start = ((), (), s32[]{:S(2)}) async-start(), calls=%async_computation | async-start | bytes 1048576 | tf_op jit(solution)/shard_map/psum | solution.py:57
  10.7 206.3 %all-gather.3.cloned.1.call-start = ((), (), s32[]{:S(2)}) async-start(), calls=%async_computation.1 | async-start | bytes 8912896 | tf_op jit(solution)/shard_map/all_gather | solution.py:99
  22.8 72.7 %copy-start.1 = (bf16[128,1024]{1,0:T(8,128)(2,1)}, bf16[128,1024]{1,0:T(8,128)(2,1)S(1)}, u32[]{:S(2)}) copy-start(bf16[128,1024]{1,0:T(8,128)(2,1)S(1)} %fusion.18) | copy-start | bytes 786436
  28.0 56.7 %copy-start.2 = (bf16[128,1024]{1,0:T(8,128)(2,1)}, bf16[128,1024]{1,0:T(8,128)(2,1)S(1)}, u32[]{:S(2)}) copy-start(bf16[128,1024]{1,0:T(8,128)(2,1)S(1)} %fusion.14) | copy-start | bytes 786436
  31.0 3.3 %copy-start.6 = (u32[32]{0:T(128)S(1)}, u32[32]{0:T(128)}, u32[]{:S(2)}) copy-start(u32[32]{0:T(128)} %constant.221) | copy-start | bytes 388
  31.0 41.0 %copy-start.4 = (s32[1,512]{1,0:T(1,128)S(1)}, s32[1,512]{1,0:T(1,128)}, u32[]{:S(2)}) copy-start(s32[1,512]{1,0:T(1,128)} %param.12) | copy-start | bytes 6148
  31.0 41.1 %copy-start.5 = (s32[4]{0:T(128)S(1)}, s32[4]{0:T(128)}, u32[]{:S(2)}) copy-start(s32[4]{0:T(128)} %param.13) | copy-start | bytes 52
  122.6 11.9 %copy-start = (f32[128,1024]{1,0:T(8,128)S(1)}, f32[128,1024]{1,0:T(8,128)}, u32[]{:S(2)}) copy-start(f32[128,1024]{1,0:T(8,128)} %all-reduce.4.cloned.1.call-done) | copy-start | bytes 1572868
  132.5 88.7 %copy-start.3 = (f32[1,15]{1,0:T(1,128)}, f32[1,15]{1,0:T(1,128)S(1)}, u32[]{:S(2)}) copy-start(f32[1,15]{1,0:T(1,128)S(1)} %fusion.71) | copy-start | bytes 184
Sparse Core Ops, SparseCore 0:
  11.9 93.5 all-reduce.3
  145.4 71.5 all-gather.2
